TPU v7x, 32 devices: a whole 2x2x4 slice. The times are simulated.
32 devices in a mesh: rep: 16 (over z, x, core), fsdp: 2 (over y).
Axes of the slice: x: 2, y: 2, z: 4, core: 2. Of those that a mesh axis runs over, the one named last changes fastest.
Arguments:
- hidden: bfloat16 [4096, 8192], P(('rep', 'fsdp')), may hold values from -6 to 6
- local_weight: bfloat16 [16, 8192, 2048], P('rep', 'fsdp'), may hold values from -0.09375 to 0.09375
- master: float32 [8192, 2048], P('fsdp', 'rep'), may hold values from -0.0625 to 0.0625
- momentum: float32 [8192, 2048], P('fsdp', 'rep'), may hold values from -0.06 to 0.06
- dither: int32 [16, 8192, 16], P('rep', 'fsdp'), may hold values from 0 to 15
Outputs:
- key_values: bfloat16 [4096, 2048], P(('rep', 'fsdp'))
- new_master: float32 [8192, 2048], P('fsdp', 'rep')
- new_momentum: float32 [8192, 2048], P('fsdp', 'rep')
- new_local: bfloat16 [16, 8192, 2048], P('rep', 'fsdp')
All inputs are finite; a program needn't handle non-finite values.
Results may differ from a plain program's by a relative error of at most 0.0067.
Values may be sent and summed in bfloat16 or wider, within the bound.
No kernel may reach another device: no remote copies, remote signals or barrier semaphores. Data moves between devices by JAX's collectives and lax.ppermute only.
A program may use at most 192 MiB of HBM per device.

v0:
```python
import math
import jax
import jax.numpy as jnp
from jax import lax
from jax.sharding import PartitionSpec as P

BLOCK = 128
momentum_keep = 0.9
outer_rate = 0.7
mix_share = 0.5


def code_block(delta, dither):
    row_count = delta.shape[0]
    blocked = delta.reshape(row_count, -1, BLOCK)
    scaling = (jnp.max(jnp.abs(blocked), axis=2, keepdims=True) + 1e-06) / 7.0
    offset = (dither.astype(jnp.float32)[:, :, None] + 0.5) / 16.0 - 0.5
    levels = jnp.clip(blocked / scaling + offset, -8.0, 7.0)
    smooth = levels - jnp.sin(2.0 * math.pi * levels) / (2.0 * math.pi)
    return (scaling * (smooth - offset)).reshape(row_count, -1)


def shards(hidden, local_weight, master, momentum, dither):
    weights = local_weight[0]
    key_values = jnp.dot(
        hidden,
        lax.all_gather(weights, "fsdp", axis=0, tiled=True),
        preferred_element_type=jnp.float32,
    ).astype(jnp.bfloat16)
    anchor = lax.all_gather(master.astype(jnp.bfloat16), "rep", axis=1, tiled=True)
    delta = anchor.astype(jnp.float32) - weights.astype(jnp.float32)
    coded = code_block(delta, dither[0]).astype(jnp.bfloat16)
    replicas = lax.axis_size("rep")
    widened = lax.optimization_barrier(coded).astype(jnp.float32)
    summed = lax.psum_scatter(widened, "rep", scatter_dimension=1, tiled=True)
    averaged = summed / replicas
    new_momentum = momentum_keep * momentum + averaged
    new_master = master - outer_rate * (averaged + momentum_keep * new_momentum)
    gathered = lax.all_gather(new_master.astype(jnp.bfloat16), "rep", axis=1, tiled=True)
    merged = mix_share * weights.astype(jnp.float32) + (1.0 - mix_share) * gathered.astype(
        jnp.float32
    )
    new_local = merged.astype(jnp.bfloat16)[None]
    return (key_values, new_master, new_momentum, new_local)


def solution(mesh):
    return jax.shard_map(
        shards,
        mesh=mesh,
        in_specs=(
            P(("rep", "fsdp"), None),
            P("rep", "fsdp", None),
            P("fsdp", "rep"),
            P("fsdp", "rep"),
            P("rep", "fsdp", None),
        ),
        out_specs=(
            P(("rep", "fsdp"), None),
            P("fsdp", "rep"),
            P("fsdp", "rep"),
            P("rep", "fsdp", None),
        ),
        check_vma=False,
    )
```

profile of v0, /device:TPU:0, one launch (start us, length us, event | category | flops | bytes accessed | tf_op | source)
XLA Modules:
  0.0 924.9 jit_solution(2626235479547939231)
XLA Ops:
  8.0 0.0 copy-start
  8.0 0.0 all-gather.5.cloned.1.call-start
  8.1 2.8 convert_element_type.37
  10.9 0.0 all-gather.5.cloned.1.call-update
  10.9 0.0 reduce-scatter.2.cloned.1.call-start
  10.9 1.0 add_bitcast_fusion
  11.9 1.9 copy.9
  13.9 130.3 %all-gather.5.cloned.1.call-done = bf16[4096,2048]{1,0:T(8,128)(2,1)} async-done(((bf16[4096,128]{1,0:T(8,128)(2,1)}), bf16[4096,2048]{1,0:T(8,128)(2,1)}) %all-gather.5.cloned.1.call-update) | async-done | bytes 16777232 | tf_op jit(solution)/shard_map/all_gather | solution.py:30
  144.2 14.2 %abs_bitcast_fusion = f32[512,8,16,128]{3,1,2,0:T(8,128)S(1)} fusion(bf16[4096,2048]{1,0:T(8,128)(2,1)} %all-gather.5.cloned.1.call-done, bf16[1,4096,2048]{2,1,0:T(8,128)(2,1)} %param.6), kind=kLoop, calls=%fused_computation.12 | loop fusion | flops 33554432 | bytes 67108864
  158.4 13.7 %copy.10 = f32[512,8,16,128]{3,2,1,0:T(8,128)} copy(f32[512,8,16,128]{3,1,2,0:T(8,128)S(1)} %abs_bitcast_fusion) | data formatting | bytes 67108864
  172.1 16.7 %reduce_max.9 = f32[4096,16]{1,0:T(8,128)} reduce(f32[4096,16,128]{2,1,0:T(8,128)} %bitcast.42, f32[]{:T(128)} %constant.5.clone.1), dimensions={2}, to_apply=%region_0.0 | reduce | flops 8323072 | bytes 33816580 | tf_op jit(solution)/shard_map/reduce_max | solution.py:16
  188.8 1.9 add_multiply_fusion
  190.7 0.0 copy-start.1
  190.7 0.0 slice-start
  190.7 0.0 slice-start.1
  190.7 17.0 %mul.31 = f32[4096,16,128]{2,1,0:T(8,128)} broadcast(f32[4096,16]{1,0:T(8,128)S(1)} %add_multiply_fusion), dimensions={0,1} | broadcast | bytes 33816576 | tf_op jit(solution)/shard_map/mul | solution.py:20
  207.7 0.0 copy-done.1
  207.7 17.0 %add.53 = f32[4096,16,128]{2,1,0:T(8,128)} broadcast(f32[4096,16]{1,0:T(8,128)S(1)} %copy-done.1), dimensions={0,1} | broadcast | bytes 33816576 | tf_op jit(solution)/shard_map/add | solution.py:18
  224.6 0.0 slice-done
  224.7 133.2 %fusion.4 = bf16[4096,2048]{1,0:T(8,128)(2,1)} fusion(f32[512,8,16,128]{3,2,1,0:T(8,128)} %bitcast.41, f32[512,8,16,128]{3,2,1,0:T(8,128)} %bitcast.40, bf16[4096,2048]{1,0:T(8,128)(2,1)} %all-gather.5.cloned.1.call-done, bf16[1,4096,2048]{2,1,0:T(8,128)(2,1)S(1)} %bitcast.39), kind=kLoop, calls=%fused_computation.8 | loop fusion | flops 100663296 | bytes 117440512 | tf_op jit(solution)/shard_map/convert_element_type | solution.py:32
  357.9 18.7 %convert_element_type.42 = f32[4096,2048]{1,0:T(8,128)} convert(bf16[4096,2048]{1,0:T(8,128)(2,1)} %fusion.4) | non-fusion elementwise | flops 8388608 | bytes 50331648 | tf_op jit(solution)/shard_map/convert_element_type | solution.py:34
  376.6 0.0 reduce-scatter.2.cloned.1.call-update
  376.6 0.0 all-gather.9.cloned.1.call-start
  376.7 0.5 all-gather.9.cloned.1.call-update
  377.2 0.2 all-gather.7.cloned.1.call-start
  377.5 327.8 %reduce-scatter.2.cloned.1.call-done = f32[4096,128]{1,0:T(8,128)} async-done(((f32[4096,2048]{1,0:T(8,128)}), f32[4096,128]{1,0:T(8,128)}) %reduce-scatter.2.cloned.1.call-update) | async-done | bytes 2097168 | tf_op jit(solution)/shard_map/reduce_scatter | solution.py:35
  705.2 5.8 fusion.11
  711.0 0.0 all-gather.7.cloned.1.call-update
  711.0 54.2 %all-gather.9.cloned.1.call-done = bf16[1,8192,2048]{2,1,0:T(8,128)(2,1)} async-done(((bf16[1,4096,2048]{2,1,0:T(8,128)(2,1)}), bf16[1,8192,2048]{2,1,0:T(8,128)(2,1)}) %all-gather.9.cloned.1.call-update) | async-done | bytes 33554448 | tf_op jit(solution)/shard_map/all_gather | solution.py:27
  765.3 14.1 %fusion.8 = bf16[128,2048]{1,0:T(8,128)(2,1)} fusion(bf16[128,8192]{1,0:T(8,128)(2,1)S(1)} %copy-done, bf16[1,8192,2048]{2,1,0:T(8,128)(2,1)} %all-gather.9.cloned.1.call-done), kind=kOutput, calls=%fused_computation.14 | convolution fusion | flops 4295229440 | bytes 36175872 | tf_op jit(solution)/shard_map/dot_general | solution.py:25
  779.4 118.2 %all-gather.7.cloned.1.call-done = bf16[4096,2048]{1,0:T(8,128)(2,1)} async-done(((bf16[4096,128]{1,0:T(8,128)(2,1)}), bf16[4096,2048]{1,0:T(8,128)(2,1)}) %all-gather.7.cloned.1.call-update) | async-done | bytes 16777232 | tf_op jit(solution)/shard_map/all_gather | solution.py:39
  897.6 19.9 %fusion.7 = bf16[1,4096,2048]{2,1,0:T(8,128)(2,1)} fusion(bf16[4096,2048]{1,0:T(8,128)(2,1)} %all-gather.7.cloned.1.call-done, bf16[1,4096,2048]{2,1,0:T(8,128)(2,1)} %param.6), kind=kLoop, calls=%fused_computation.13 | loop fusion | flops 41943040 | bytes 50331648 | tf_op jit(solution)/shard_map/broadcast_in_dim | solution.py:43
  (7 shorter events, 0.0 us)
Async XLA Ops:
  8.0 757.3 %copy-start = (bf16[128,8192]{1,0:T(8,128)(2,1)S(1)}, bf16[128,8192]{1,0:T(8,128)(2,1)}, u32[]{:S(2)}) copy-start(bf16[128,8192]{1,0:T(8,128)(2,1)} %param.5) | copy-start | bytes 6291460
  8.0 136.2 %all-gather.5.cloned.1.call-start = ((), (), s32[]{:S(2)}) async-start(), calls=%async_computation.1 | async-start | bytes 17825792 | tf_op jit(solution)/shard_map/all_gather | solution.py:30
  10.9 694.3 %reduce-scatter.2.cloned.1.call-start = ((), (), s32[]{:S(2)}) async-start(), calls=%async_computation.2 | async-start | bytes 35651584 | tf_op jit(solution)/shard_map/reduce_scatter | solution.py:35
  190.7 17.0 %copy-start.1 = (f32[4096,16]{1,0:T(8,128)S(1)}, f32[4096,16]{1,0:T(8,128)}, u32[]{:S(2)}) copy-start(f32[4096,16]{1,0:T(8,128)} %copy.9) | copy-start | bytes 786436
  190.7 34.0 %slice-start = ((s8[16777216]{0:T(1024)(128)(4,1)}), s8[4194304]{0:T(1024)(128)(4,1)S(1)}, s32[]{:S(2)}) async-start(s8[16777216]{0:T(1024)(128)(4,1)} %bitcast.38), calls=%async_computation.5 | async-start | bytes 8388608
  190.7 34.0 %slice-start.1 = ((s8[16777216]{0:T(1024)(128)(4,1)}), s8[4194304]{0:T(1024)(128)(4,1)S(1)}, s32[]{:S(2)}) async-start(s8[16777216]{0:T(1024)(128)(4,1)} %bitcast.38), calls=%async_computation.6 | async-start | bytes 8388608
  207.7 17.0 %slice-start.2 = ((s8[16777216]{0:T(1024)(128)(4,1)}), s8[4194304]{0:T(1024)(128)(4,1)S(1)}, s32[]{:S(2)}) async-start(s8[16777216]{0:T(1024)(128)(4,1)} %bitcast.38), calls=%async_computation.7 | async-start | bytes 8388608
  207.7 17.0 %slice-start.3 = ((s8[16777216]{0:T(1024)(128)(4,1)}), s8[4194304]{0:T(1024)(128)(4,1)S(1)}, s32[]{:S(2)}) async-start(s8[16777216]{0:T(1024)(128)(4,1)} %bitcast.38), calls=%async_computation.8 | async-start | bytes 8388608
  376.6 388.6 %all-gather.9.cloned.1.call-start = ((), (), s32[]{:S(2)}) async-start(), calls=%async_computation.4 | async-start | bytes 50331648 | tf_op jit(solution)/shard_map/all_gather | solution.py:27
  377.2 520.4 %all-gather.7.cloned.1.call-start = ((), (), s32[]{:S(2)}) async-start(), calls=%async_computation.3 | async-start | bytes 17825792 | tf_op jit(solution)/shard_map/all_gather | solution.py:39
Sparse Core Ops, SparseCore 0:
  11.5 132.5 all-gather.4
  376.8 328.4 reduce-scatter.1
Sparse Core Ops, SparseCore 1:
  378.7 386.6 all-gather.8
  767.9 129.7 all-gather.6
where the time goes:
time: 925 us
  waiting for transfers between devices  631 us (68%)
  other arithmetic  214 us (23%)
  local copies, waits for them, and re-layouts  49.6 us (5%)
  between operations  15.6 us (2%)
  matrix products  14.1 us (2%)
    reduce_scatter x1, waiting for transfers between devices, shards(): summed = lax.psum_scatter(widened, 'rep', scatter_dimension=1, tiled=True)  328 us
    convert_element_type x1, other arithmetic, shards(): coded = code_block(delta, dither[0]).astype(jnp.bfloat16)  133 us
    all_gather x1, waiting for transfers between devices, shards(): lax.all_gather(master.astype(jnp.bfloat16), 'rep', axis=1, tiled=True)  130 us
    all_gather x1, waiting for transfers between devices, shards(): lax.all_gather(new_master.astype(jnp.bfloat16), 'rep', axis=1, tiled=True)  118 us
    all_gather x1, waiting for transfers between devices, shards(): lax.all_gather(weights, 'fsdp', axis=0, tiled=True)  54.2 us
    broadcast_in_dim x1, other arithmetic, shards(): new_local = merged.astype(jnp.bfloat16)[None]  19.9 us
    convert_element_type x1, other arithmetic, shards(): widened = lax.optimization_barrier(coded).astype(jnp.float32)  18.7 us
  transfers between devices with their start and end apart: 4, of which 4 were waited for; matrix products, arithmetic and copies ran while one was open for 2% of the time, Pallas kernels for 0%

commit v1 on v0

--- a/solution.py
+++ b/solution.py
@@ -8,6 +8,12 @@
 momentum_keep = 0.9
 outer_rate = 0.7
 mix_share = 0.5
+
+
+def joined_along(pieces, dim):
+    dims = list(pieces.shape[1:])
+    dims[dim] *= pieces.shape[0]
+    return jnp.moveaxis(pieces, 0, dim).reshape(dims)
 
 
 def code_block(delta, dither):
@@ -27,7 +33,20 @@
         lax.all_gather(weights, "fsdp", axis=0, tiled=True),
         preferred_element_type=jnp.float32,
     ).astype(jnp.bfloat16)
-    anchor = lax.all_gather(master.astype(jnp.bfloat16), "rep", axis=1, tiled=True)
+    x = master.astype(jnp.bfloat16)
+    devices = lax.axis_size("rep")
+    pairs = [(i, (i + 1) % devices) for i in range(devices)]
+    back = [(b, a) for a, b in pairs]
+    lower, upper = ([], [])
+    for step in range(devices - 1):
+        if step % 2 == 0:
+            lower.append(lax.ppermute(lower[-1] if lower else x, "rep", pairs))
+        else:
+            upper.append(lax.ppermute(upper[-1] if upper else x, "rep", back))
+    blocks = jnp.stack([*lower[::-1], x, *upper])
+    shift = lax.axis_index("rep") - len(lower)
+    blocks = blocks[(jnp.arange(devices) - shift) % devices]
+    anchor = joined_along(blocks, 1)
     delta = anchor.astype(jnp.float32) - weights.astype(jnp.float32)
     coded = code_block(delta, dither[0]).astype(jnp.bfloat16)
     replicas = lax.axis_size("rep")

time: 925 us -> 956 us (1.034)
  starting transfers between devices: 0.35 us -> 93 us
  waiting for transfers between devices: 631 us -> 552 us
  local copies, waits for them, and re-layouts: 49.6 us -> 64.1 us
    all_gather x1 -> x0, waiting for transfers between devices: 130 us -> none  [shards(): lax.all_gather(master.astype(jnp.bfloat16), 'rep', axis=1, tiled=True)]
    ppermute x0 -> x15, starting transfers between devices: none -> 92.7 us  [the longest x8 85.1 us: shards(): lower.append(lax.ppermute(lower[-1] if lower else x, 'rep', pairs))]
    ppermute x0 -> x15, waiting for transfers between devices: none -> 49.2 us  [the longest x8 49.2 us: shards(): lower.append(lax.ppermute(lower[-1] if lower else x, 'rep', pairs))]
    unnamed x13 -> x51, local copies, waits for them, and re-layouts: 13.7 us -> 50 us
    mul x1 -> x0, local copies, waits for them, and re-layouts: 17 us -> none  [code_block(): return (scaling * (smooth - offset)).reshape(row_count, -1)]
    add x1 -> x0, local copies, waits for them, and re-layouts: 17 us -> none  [code_block(): levels = jnp.clip(blocked / scaling + offset, -8.0, 7.0)]
    gather x0 -> x1, local copies, waits for them, and re-layouts: none -> 13.1 us  [shards(): blocks = blocks[(jnp.arange(devices) - shift) % devices]]
  transfers between devices with their start and end apart: 4 -> 18, of which waited for: 4 -> 9; matrix products, arithmetic and copies ran while one was open for 2% -> 9% of each run, Pallas kernels for 0% -> 0%
where the time goes in v1:
time: 956 us; the launch traced here: 955 us
  waiting for transfers between devices  552 us (58%)
  other arithmetic  217 us (23%)
  starting transfers between devices  93 us (10%)
  local copies, waits for them, and re-layouts  64.1 us (7%)
  between operations  15.7 us (2%)
  matrix products  14.1 us (1%)
    reduce_scatter x1, waiting for transfers between devices, shards(): summed = lax.psum_scatter(widened, 'rep', scatter_dimension=1, tiled=True)  330 us
    convert_element_type x1, other arithmetic, shards(): coded = code_block(delta, dither[0]).astype(jnp.bfloat16)  128 us
    all_gather x1, waiting for transfers between devices, shards(): lax.all_gather(new_master.astype(jnp.bfloat16), 'rep', axis=1, tiled=True)  118 us
    ppermute x8, starting transfers between devices, shards(): lower.append(lax.ppermute(lower[-1] if lower else x, 'rep', pairs))  85.1 us
    all_gather x1, waiting for transfers between devices, shards(): lax.all_gather(weights, 'fsdp', axis=0, tiled=True)  54.2 us
    unnamed x51, local copies, waits for them, and re-layouts  50 us
    ppermute x8, waiting for transfers between devices, shards(): lower.append(lax.ppermute(lower[-1] if lower else x, 'rep', pairs))  49.2 us
    reduce_max x1, other arithmetic, code_block(): scaling = (jnp.max(jnp.abs(blocked), axis=2, keepdims=True) + 1e-06) / 7.0  21.9 us
  transfers between devices with their start and end apart: 18, of which 9 were waited for; matrix products, arithmetic and copies ran while one was open for 9% of the time, Pallas kernels for 0%

profile of v1, /device:TPU:0, one launch (start us, length us, event | category | flops | bytes accessed | tf_op | source)
XLA Modules:
  0.0 955.3 jit_solution(3120270336829555901)
XLA Ops:
  8.1 1.8 convert_element_type.50
  10.4 17.4 %collective-permute-done = bf16[4096,128]{1,0:T(8,128)(2,1)S(1)} collective-permute-done((bf16[4096,128]{1,0:T(8,128)(2,1)S(1)}, bf16[4096,128]{1,0:T(8,128)(2,1)S(1)}, u32[]{:S(2)}, u32[]{:S(2)}) %collective-permute-start) | collective-permute-done | bytes 1048608 | tf_op jit(solution)/shard_map/ppermute | solution.py:43
  27.9 4.4 collective-permute-start.8
  32.3 12.6 %collective-permute-done.1 = bf16[4096,128]{1,0:T(8,128)(2,1)S(1)} collective-permute-done((bf16[4096,128]{1,0:T(8,128)(2,1)S(1)}, bf16[4096,128]{1,0:T(8,128)(2,1)S(1)}, u32[]{:S(2)}, u32[]{:S(2)}) %collective-permute-start.1) | collective-permute-done | bytes 1048608 | tf_op jit(solution)/shard_map/ppermute | solution.py:43
  44.9 5.3 collective-permute-start.2
  51.2 10.7 %collective-permute-done.2 = bf16[4096,128]{1,0:T(8,128)(2,1)S(1)} collective-permute-done((bf16[4096,128]{1,0:T(8,128)(2,1)S(1)}, bf16[4096,128]{1,0:T(8,128)(2,1)S(1)}, u32[]{:S(2)}, u32[]{:S(2)}) %collective-permute-start.2) | collective-permute-done | bytes 1048608 | tf_op jit(solution)/shard_map/ppermute | solution.py:43
  61.9 13.8 %collective-permute-start.3 = (bf16[4096,128]{1,0:T(8,128)(2,1)S(1)}, bf16[4096,128]{1,0:T(8,128)(2,1)S(1)}, u32[]{:S(2)}, u32[]{:S(2)}) collective-permute-start(bf16[4096,128]{1,0:T(8,128)(2,1)S(1)} %collective-permute-done.2), channel_id=1, source_target_pairs={{0,2},{2,4},{4,6},{6,8},{8,10},{10,12},{12,14},{14,16},{16,18},{18... | collective-permute-start | bytes 3145736 | tf_op jit(solution)/shard_map/ppermute | solution.py:43
  76.7 3.8 collective-permute-done.3
  80.4 20.0 %collective-permute-start.4 = (bf16[4096,128]{1,0:T(8,128)(2,1)S(1)}, bf16[4096,128]{1,0:T(8,128)(2,1)S(1)}, u32[]{:S(2)}, u32[]{:S(2)}) collective-permute-start(bf16[4096,128]{1,0:T(8,128)(2,1)S(1)} %collective-permute-done.3), channel_id=1, source_target_pairs={{0,2},{2,4},{4,6},{6,8},{8,10},{10,12},{12,14},{14,16},{16,18},{18... | collective-permute-start | bytes 3145736 | tf_op jit(solution)/shard_map/ppermute | solution.py:43
  101.4 2.3 collective-permute-done.4
  103.7 21.5 %collective-permute-start.5 = (bf16[4096,128]{1,0:T(8,128)(2,1)S(1)}, bf16[4096,128]{1,0:T(8,128)(2,1)}, u32[]{:S(2)}, u32[]{:S(2)}) collective-permute-start(bf16[4096,128]{1,0:T(8,128)(2,1)S(1)} %collective-permute-done.4), channel_id=1, source_target_pairs={{0,2},{2,4},{4,6},{6,8},{8,10},{10,12},{12,14},{14,16},{16,18},{18... | collective-permute-start | bytes 3145736 | tf_op jit(solution)/shard_map/ppermute | solution.py:43
  125.2 2.4 collective-permute-done.5
  127.6 21.4 %collective-permute-start.6 = (bf16[4096,128]{1,0:T(8,128)(2,1)}, bf16[4096,128]{1,0:T(8,128)(2,1)}, u32[]{:S(2)}, u32[]{:S(2)}) collective-permute-start(bf16[4096,128]{1,0:T(8,128)(2,1)} %collective-permute-done.5), channel_id=1, source_target_pairs={{0,2},{2,4},{4,6},{6,8},{8,10},{10,12},{12,14},{14,16},{16,18},{18... | collective-permute-start | bytes 3145736 | tf_op jit(solution)/shard_map/ppermute | solution.py:43
  149.0 18.7 %convert_bitcast_fusion.1 = f32[512,8,16,128]{3,1,2,0:T(8,128)} fusion(bf16[1,4096,2048]{2,1,0:T(8,128)(2,1)} %param.6), kind=kLoop, calls=%fused_computation.2 | loop fusion | flops 8388608 | bytes 50331648
  167.7 2.6 collective-permute-start.7
  170.4 27.7 %copy.12 = f32[512,8,16,128]{3,2,1,0:T(8,128)} copy(f32[512,8,16,128]{3,1,2,0:T(8,128)} %convert_bitcast_fusion.1) | data formatting | bytes 67108864
  198.2 3.0 collective-permute-start.14
  202.3 2.3 bitcast_dynamic-update-slice_fusion.14
  204.5 2.3 bitcast_dynamic-update-slice_fusion.13
  212.0 1.1 bitcast_dynamic-update-slice_fusion.7
  216.2 2.3 bitcast_dynamic-update-slice_fusion.3
  218.4 2.3 bitcast_dynamic-update-slice_fusion.2
  222.8 13.1 %gather_fusion = bf16[16,4096,128]{2,1,0:T(8,128)(2,1)} fusion(bf16[16,4096,128]{2,1,0:T(8,128)(2,1)} %bitcast_dynamic-update-slice_fusion, s32[1024]{0:T(1024)S(1)} %pad_clamp_fusion), kind=kCustom, calls=%fused_computation | custom fusion | bytes 33554496 | tf_op jit(solution)/shard_map/gather | solution.py:48
  235.9 21.9 %abs_reduce_fusion = f32[4096,16]{0,1:T(8,128)S(1)} fusion(f32[4096,16,128]{2,1,0:T(8,128)} %bitcast.72, bf16[16,4096,128]{2,1,0:T(8,128)(2,1)} %gather_fusion), kind=kLoop, calls=%fused_computation.10 | loop fusion | flops 33488896 | bytes 50593792 | tf_op jit(solution)/shard_map/reduce_max | solution.py:22
  257.8 128.5 %copy_bitcast_fusion = bf16[4096,2048]{1,0:T(8,128)(2,1)} fusion(f32[4096,16]{0,1:T(8,128)S(1)} %add_bitcast_fusion, f32[4096,16,128]{2,1,0:T(8,128)} %bitcast.73, bf16[16,4096,128]{2,1,0:T(8,128)(2,1)S(1)} %copy-done.1, f32[4096,16]{0,1:T(8,128)S(1)} %add_multiply_fusion), kind=kLoop, calls=%fused_computation.12 | loop fusion | flops 92274688 | bytes 67633152 | tf_op jit(solution)/shard_map/convert_element_type | solution.py:51
  386.3 18.7 %convert_element_type.58 = f32[4096,2048]{1,0:T(8,128)} convert(bf16[4096,2048]{1,0:T(8,128)(2,1)} %copy_bitcast_fusion) | non-fusion elementwise | flops 8388608 | bytes 50331648 | tf_op jit(solution)/shard_map/convert_element_type | solution.py:53
  405.9 329.7 %reduce-scatter.2.cloned.1.call-done = f32[4096,128]{1,0:T(8,128)} async-done(((f32[4096,2048]{1,0:T(8,128)}), f32[4096,128]{1,0:T(8,128)}) %reduce-scatter.2.cloned.1.call-update) | async-done | bytes 2097168 | tf_op jit(solution)/shard_map/reduce_scatter | solution.py:54
  735.6 5.8 fusion.12
  741.4 54.2 %all-gather.6.cloned.1.call-done = bf16[1,8192,2048]{2,1,0:T(8,128)(2,1)} async-done(((bf16[1,4096,2048]{2,1,0:T(8,128)(2,1)}), bf16[1,8192,2048]{2,1,0:T(8,128)(2,1)}) %all-gather.6.cloned.1.call-update) | async-done | bytes 33554448 | tf_op jit(solution)/shard_map/all_gather | solution.py:33
  795.6 14.1 %fusion.7 = bf16[128,2048]{1,0:T(8,128)(2,1)} fusion(bf16[128,8192]{1,0:T(8,128)(2,1)S(1)} %copy-done, bf16[1,8192,2048]{2,1,0:T(8,128)(2,1)} %all-gather.6.cloned.1.call-done), kind=kOutput, calls=%fused_computation.14 | convolution fusion | flops 4295229440 | bytes 36175872 | tf_op jit(solution)/shard_map/dot_general | solution.py:31
  809.7 118.2 %all-gather.4.cloned.1.call-done = bf16[4096,2048]{1,0:T(8,128)(2,1)} async-done(((bf16[4096,128]{1,0:T(8,128)(2,1)}), bf16[4096,2048]{1,0:T(8,128)(2,1)}) %all-gather.4.cloned.1.call-update) | async-done | bytes 16777232 | tf_op jit(solution)/shard_map/all_gather | solution.py:58
  928.0 19.9 %fusion.5 = bf16[1,4096,2048]{2,1,0:T(8,128)(2,1)} fusion(bf16[4096,2048]{1,0:T(8,128)(2,1)} %all-gather.4.cloned.1.call-done, bf16[1,4096,2048]{2,1,0:T(8,128)(2,1)} %param.6), kind=kLoop, calls=%fused_computation.11 | loop fusion | flops 41943040 | bytes 50331648 | tf_op jit(solution)/shard_map/broadcast_in_dim | solution.py:62
  (73 shorter events, 16.0 us)
Async XLA Ops:
  8.0 787.6 %copy-start = (bf16[128,8192]{1,0:T(8,128)(2,1)S(1)}, bf16[128,8192]{1,0:T(8,128)(2,1)}, u32[]{:S(2)}) copy-start(bf16[128,8192]{1,0:T(8,128)(2,1)} %param.5) | copy-start | bytes 6291460
  8.0 727.6 %reduce-scatter.2.cloned.1.call-start = ((), (), s32[]{:S(2)}) async-start(), calls=%async_computation.1 | async-start | bytes 35651584 | tf_op jit(solution)/shard_map/reduce_scatter | solution.py:54
  9.9 18.0 %collective-permute-start = (bf16[4096,128]{1,0:T(8,128)(2,1)S(1)}, bf16[4096,128]{1,0:T(8,128)(2,1)S(1)}, u32[]{:S(2)}, u32[]{:S(2)}) collective-permute-start(bf16[4096,128]{1,0:T(8,128)(2,1)S(1)} %convert_element_type.50), channel_id=1, source_target_pairs={{0,2},{2,4},{4,6},{6,8},{8,10},{10,12},{12,14},{14,16},{16,18},{18... | collective-permute-start | bytes 3145736 | tf_op jit(solution)/shard_map/ppermute | solution.py:43
  27.9 17.0 %collective-permute-start.1 = (bf16[4096,128]{1,0:T(8,128)(2,1)S(1)}, bf16[4096,128]{1,0:T(8,128)(2,1)S(1)}, u32[]{:S(2)}, u32[]{:S(2)}) collective-permute-start(bf16[4096,128]{1,0:T(8,128)(2,1)S(1)} %collective-permute-done), channel_id=1, source_target_pairs={{0,2},{2,4},{4,6},{6,8},{8,10},{10,12},{12,14},{14,16},{16,18},{18... | collective-permute-start | bytes 3145736 | tf_op jit(solution)/shard_map/ppermute | solution.py:43
  27.9 22.4 %collective-permute-start.8 = (bf16[4096,128]{1,0:T(8,128)(2,1)S(1)}, bf16[4096,128]{1,0:T(8,128)(2,1)S(1)}, u32[]{:S(2)}, u32[]{:S(2)}) collective-permute-start(bf16[4096,128]{1,0:T(8,128)(2,1)S(1)} %convert_element_type.50), channel_id=1, source_target_pairs={{2,0},{4,2},{6,4},{8,6},{10,8},{12,10},{14,12},{16,14},{18,16},{20... | collective-permute-start | bytes 3145736 | tf_op jit(solution)/shard_map/ppermute | solution.py:45
  44.9 30.8 %copy-start.5 = (bf16[4096,128]{1,0:T(8,128)(2,1)}, bf16[4096,128]{1,0:T(8,128)(2,1)S(1)}, u32[]{:S(2)}) copy-start(bf16[4096,128]{1,0:T(8,128)(2,1)S(1)} %collective-permute-done.1) | copy-start | bytes 3145732
  44.9 17.0 %collective-permute-start.2 = (bf16[4096,128]{1,0:T(8,128)(2,1)S(1)}, bf16[4096,128]{1,0:T(8,128)(2,1)S(1)}, u32[]{:S(2)}, u32[]{:S(2)}) collective-permute-start(bf16[4096,128]{1,0:T(8,128)(2,1)S(1)} %collective-permute-done.1), channel_id=1, source_target_pairs={{0,2},{2,4},{4,6},{6,8},{8,10},{10,12},{12,14},{14,16},{16,18},{18... | collective-permute-start | bytes 3145736 | tf_op jit(solution)/shard_map/ppermute | solution.py:43
  51.2 24.5 %collective-permute-start.9 = (bf16[4096,128]{1,0:T(8,128)(2,1)S(1)}, bf16[4096,128]{1,0:T(8,128)(2,1)S(1)}, u32[]{:S(2)}, u32[]{:S(2)}) collective-permute-start(bf16[4096,128]{1,0:T(8,128)(2,1)S(1)} %collective-permute-done.8), channel_id=1, source_target_pairs={{2,0},{4,2},{6,4},{8,6},{10,8},{12,10},{14,12},{16,14},{18,16},{20... | collective-permute-start | bytes 3145736 | tf_op jit(solution)/shard_map/ppermute | solution.py:45
  61.9 38.5 %copy-start.9 = (bf16[4096,128]{1,0:T(8,128)(2,1)}, bf16[4096,128]{1,0:T(8,128)(2,1)S(1)}, u32[]{:S(2)}) copy-start(bf16[4096,128]{1,0:T(8,128)(2,1)S(1)} %collective-permute-done.2) | copy-start | bytes 3145732
  61.9 18.5 %collective-permute-start.3 = (bf16[4096,128]{1,0:T(8,128)(2,1)S(1)}, bf16[4096,128]{1,0:T(8,128)(2,1)S(1)}, u32[]{:S(2)}, u32[]{:S(2)}) collective-permute-start(bf16[4096,128]{1,0:T(8,128)(2,1)S(1)} %collective-permute-done.2), channel_id=1, source_target_pairs={{0,2},{2,4},{4,6},{6,8},{8,10},{10,12},{12,14},{14,16},{16,18},{18... | collective-permute-start | bytes 3145736 | tf_op jit(solution)/shard_map/ppermute | solution.py:43
  75.7 24.7 %collective-permute-start.10 = (bf16[4096,128]{1,0:T(8,128)(2,1)S(1)}, bf16[4096,128]{1,0:T(8,128)(2,1)S(1)}, u32[]{:S(2)}, u32[]{:S(2)}) collective-permute-start(bf16[4096,128]{1,0:T(8,128)(2,1)S(1)} %collective-permute-done.9), channel_id=1, source_target_pairs={{2,0},{4,2},{6,4},{8,6},{10,8},{12,10},{14,12},{16,14},{18,16},{20... | collective-permute-start | bytes 3145736 | tf_op jit(solution)/shard_map/ppermute | solution.py:45
  80.4 44.8 %copy-start.13 = (bf16[4096,128]{1,0:T(8,128)(2,1)}, bf16[4096,128]{1,0:T(8,128)(2,1)S(1)}, u32[]{:S(2)}) copy-start(bf16[4096,128]{1,0:T(8,128)(2,1)S(1)} %collective-permute-done.3) | copy-start | bytes 3145732
  80.4 23.3 %collective-permute-start.4 = (bf16[4096,128]{1,0:T(8,128)(2,1)S(1)}, bf16[4096,128]{1,0:T(8,128)(2,1)S(1)}, u32[]{:S(2)}, u32[]{:S(2)}) collective-permute-start(bf16[4096,128]{1,0:T(8,128)(2,1)S(1)} %collective-permute-done.3), channel_id=1, source_target_pairs={{0,2},{2,4},{4,6},{6,8},{8,10},{10,12},{12,14},{14,16},{16,18},{18... | collective-permute-start | bytes 3145736 | tf_op jit(solution)/shard_map/ppermute | solution.py:43
  100.5 24.7 %collective-permute-start.11 = (bf16[4096,128]{1,0:T(8,128)(2,1)S(1)}, bf16[4096,128]{1,0:T(8,128)(2,1)}, u32[]{:S(2)}, u32[]{:S(2)}) collective-permute-start(bf16[4096,128]{1,0:T(8,128)(2,1)S(1)} %collective-permute-done.10), channel_id=1, source_target_pairs={{2,0},{4,2},{6,4},{8,6},{10,8},{12,10},{14,12},{16,14},{18,16},{20... | collective-permute-start | bytes 3145736 | tf_op jit(solution)/shard_map/ppermute | solution.py:45
  103.7 21.5 %copy-start.15 = (bf16[4096,128]{1,0:T(8,128)(2,1)}, bf16[4096,128]{1,0:T(8,128)(2,1)S(1)}, u32[]{:S(2)}) copy-start(bf16[4096,128]{1,0:T(8,128)(2,1)S(1)} %collective-permute-done.4) | copy-start | bytes 3145732
  103.7 23.9 %collective-permute-start.5 = (bf16[4096,128]{1,0:T(8,128)(2,1)S(1)}, bf16[4096,128]{1,0:T(8,128)(2,1)}, u32[]{:S(2)}, u32[]{:S(2)}) collective-permute-start(bf16[4096,128]{1,0:T(8,128)(2,1)S(1)} %collective-permute-done.4), channel_id=1, source_target_pairs={{0,2},{2,4},{4,6},{6,8},{8,10},{10,12},{12,14},{14,16},{16,18},{18... | collective-permute-start | bytes 3145736 | tf_op jit(solution)/shard_map/ppermute | solution.py:43
  125.2 42.5 %collective-permute-start.12 = (bf16[4096,128]{1,0:T(8,128)(2,1)}, bf16[4096,128]{1,0:T(8,128)(2,1)}, u32[]{:S(2)}, u32[]{:S(2)}) collective-permute-start(bf16[4096,128]{1,0:T(8,128)(2,1)} %collective-permute-done.11), channel_id=1, source_target_pairs={{2,0},{4,2},{6,4},{8,6},{10,8},{12,10},{14,12},{16,14},{18,16},{20... | collective-permute-start | bytes 3145736 | tf_op jit(solution)/shard_map/ppermute | solution.py:45
  127.6 40.1 %collective-permute-start.6 = (bf16[4096,128]{1,0:T(8,128)(2,1)}, bf16[4096,128]{1,0:T(8,128)(2,1)}, u32[]{:S(2)}, u32[]{:S(2)}) collective-permute-start(bf16[4096,128]{1,0:T(8,128)(2,1)} %collective-permute-done.5), channel_id=1, source_target_pairs={{0,2},{2,4},{4,6},{6,8},{8,10},{10,12},{12,14},{14,16},{16,18},{18... | collective-permute-start | bytes 3145736 | tf_op jit(solution)/shard_map/ppermute | solution.py:43
  167.7 30.5 %collective-permute-start.13 = (bf16[4096,128]{1,0:T(8,128)(2,1)}, bf16[4096,128]{1,0:T(8,128)(2,1)S(1)}, u32[]{:S(2)}, u32[]{:S(2)}) collective-permute-start(bf16[4096,128]{1,0:T(8,128)(2,1)} %collective-permute-done.12), channel_id=1, source_target_pairs={{2,0},{4,2},{6,4},{8,6},{10,8},{12,10},{14,12},{16,14},{18,16},{20... | collective-permute-start | bytes 3145736 | tf_op jit(solution)/shard_map/ppermute | solution.py:45
  167.7 33.5 %collective-permute-start.7 = (bf16[4096,128]{1,0:T(8,128)(2,1)}, bf16[4096,128]{1,0:T(8,128)(2,1)S(1)}, u32[]{:S(2)}, u32[]{:S(2)}) collective-permute-start(bf16[4096,128]{1,0:T(8,128)(2,1)} %collective-permute-done.6), channel_id=1, source_target_pairs={{0,2},{2,4},{4,6},{6,8},{8,10},{10,12},{12,14},{14,16},{16,18},{18... | collective-permute-start | bytes 3145736 | tf_op jit(solution)/shard_map/ppermute | solution.py:43
  170.4 27.8 %copy-start.17 = (s32[1,4096,16]{1,2,0:T(8,128)S(1)}, s32[1,4096,16]{1,2,0:T(8,128)}, u32[]{:S(2)}) copy-start(s32[1,4096,16]{1,2,0:T(8,128)} %param.9) | copy-start | bytes 786436
  170.4 36.4 %copy-start.16 = (bf16[4096,128]{1,0:T(8,128)(2,1)S(1)}, bf16[4096,128]{1,0:T(8,128)(2,1)}, u32[]{:S(2)}) copy-start(bf16[4096,128]{1,0:T(8,128)(2,1)} %copy-done.15) | copy-start | bytes 3145732
  170.4 37.4 %copy-start.14 = (bf16[4096,128]{1,0:T(8,128)(2,1)S(1)}, bf16[4096,128]{1,0:T(8,128)(2,1)}, u32[]{:S(2)}) copy-start(bf16[4096,128]{1,0:T(8,128)(2,1)} %copy-done.13) | copy-start | bytes 3145732
  170.4 38.5 %copy-start.10 = (bf16[4096,128]{1,0:T(8,128)(2,1)S(1)}, bf16[4096,128]{1,0:T(8,128)(2,1)}, u32[]{:S(2)}) copy-start(bf16[4096,128]{1,0:T(8,128)(2,1)} %copy-done.9) | copy-start | bytes 3145732
  170.4 39.5 %copy-start.6 = (bf16[4096,128]{1,0:T(8,128)(2,1)S(1)}, bf16[4096,128]{1,0:T(8,128)(2,1)}, u32[]{:S(2)}) copy-start(bf16[4096,128]{1,0:T(8,128)(2,1)} %copy-done.5) | copy-start | bytes 3145732
  198.1 14.9 %copy-start.4 = (bf16[4096,128]{1,0:T(8,128)(2,1)S(1)}, bf16[4096,128]{1,0:T(8,128)(2,1)}, u32[]{:S(2)}) copy-start(bf16[4096,128]{1,0:T(8,128)(2,1)} %copy-done.3) | copy-start | bytes 3145732
  198.1 16.0 %copy-start.8 = (bf16[4096,128]{1,0:T(8,128)(2,1)S(1)}, bf16[4096,128]{1,0:T(8,128)(2,1)}, u32[]{:S(2)}) copy-start(bf16[4096,128]{1,0:T(8,128)(2,1)} %copy-done.7) | copy-start | bytes 3145732
  198.1 17.0 %copy-start.12 = (bf16[4096,128]{1,0:T(8,128)(2,1)S(1)}, bf16[4096,128]{1,0:T(8,128)(2,1)}, u32[]{:S(2)}) copy-start(bf16[4096,128]{1,0:T(8,128)(2,1)} %copy-done.11) | copy-start | bytes 3145732
  198.2 23.5 %collective-permute-start.14 = (bf16[4096,128]{1,0:T(8,128)(2,1)S(1)}, bf16[4096,128]{1,0:T(8,128)(2,1)S(1)}, u32[]{:S(2)}, u32[]{:S(2)}) collective-permute-start(bf16[4096,128]{1,0:T(8,128)(2,1)S(1)} %collective-permute-done.13), channel_id=1, source_target_pairs={{2,0},{4,2},{6,4},{8,6},{10,8},{12,10},{14,12},{16,14},{18,16},{20... | collective-permute-start | bytes 3145736 | tf_op jit(solution)/shard_map/ppermute | solution.py:45
  235.9 22.0 %copy-start.1 = (bf16[16,4096,128]{2,1,0:T(8,128)(2,1)S(1)}, bf16[16,4096,128]{2,1,0:T(8,128)(2,1)}, u32[]{:S(2)}) copy-start(bf16[16,4096,128]{2,1,0:T(8,128)(2,1)} %gather_fusion) | copy-start | bytes 50331652
  405.1 390.6 %all-gather.6.cloned.1.call-start = ((), (), s32[]{:S(2)}) async-start(), calls=%async_computation.3 | async-start | bytes 50331648 | tf_op jit(solution)/shard_map/all_gather | solution.py:33
  405.7 522.3 %all-gather.4.cloned.1.call-start = ((), (), s32[]{:S(2)}) async-start(), calls=%async_computation.2 | async-start | bytes 17825792 | tf_op jit(solution)/shard_map/all_gather | solution.py:58
  (4 other events, 16.8 us)
Sparse Core Ops, SparseCore 0:
  405.2 330.3 reduce-scatter.1
Sparse Core Ops, SparseCore 1:
  407.1 388.5 all-gather.5
  798.2 129.7 all-gather.3
